TPU v7x, 256 devices: a whole 4x4x8 slice. The times are simulated.
256 devices in a mesh: shard: 64 (over x, y_hi, z), tensor: 4 (over y_lo, core).
Axes of the slice: x: 4, y: 4 (y_hi: 2, y_lo: 2; y = y_hi * 2 + y_lo), z: 8, core: 2. Of those that a mesh axis runs over, the one named last changes fastest.
Arguments:
- gradient: bfloat16 [768, 3072], P('shard', 'tensor'), may hold values from -0.47851562 to 0.47851562
- moment: float32 [768, 3072], P('shard', 'tensor'), may hold values from -0.48 to 0.48
- second_moment: float32 [768, 3072], P('shard', 'tensor'), may hold values from 0.0001 to 0.01
- stat_left: float32 [768, 768], P('shard', 'tensor'), as said below
- stat_right: float32 [3072, 3072], P('shard', 'tensor'), as said below
- basis_left: float32 [768, 768], P('shard', 'tensor'), as said below
- basis_right: float32 [3072, 3072], P('shard', 'tensor'), as said below
Outputs:
- update: float32 [768, 3072], P('shard', 'tensor')
- moment_new: float32 [768, 3072], P('shard', 'tensor')
- second_new: float32 [768, 3072], P('shard', 'tensor')
- stat_left_new: float32 [768, 768], P('shard', 'tensor')
- stat_right_new: float32 [3072, 3072], P('shard', 'tensor')
- basis_left_new: float32 [768, 768], P('shard', 'tensor')
- basis_right_new: float32 [3072, 3072], P('shard', 'tensor')
Inputs may be any that keep to these rules, and one draw needn't show every extreme that they name: `stat_left`: a symmetric matrix. `stat_right`: a symmetric matrix. `basis_left`: a square matrix of full rank. `basis_right`: a square matrix of full rank.
All inputs are finite; a program needn't handle non-finite values.
Results may differ from a plain program's by a relative error of at most 0.0018.
The roundings to bfloat16 on the way count: a program that leaves them out, or rounds other values in their place, can miss the bound.
Values may be sent and summed in bfloat16 or wider, within the bound.
No kernel may reach another device: no remote copies, remote signals or barrier semaphores. Data moves between devices by JAX's collectives and lax.ppermute only.
A program may use at most 64 MiB of HBM per device.

v0:
```python
import jax
import jax.numpy as jnp
from jax import lax
from jax.sharding import PartitionSpec as P

NS_ITERS = 2


def broadcast(array, axis, root):
    mine = lax.axis_index(axis) == root
    return lax.psum(jnp.where(mine, array, jnp.zeros_like(array)), axis)


def matmul(first_operand, second_operand):
    return jnp.dot(first_operand, second_operand, preferred_element_type=jnp.float32)


def contract_rows(first_operand, second_operand):
    return lax.dot_general(
        first_operand, second_operand, (((0,), (0,)), ((), ())), preferred_element_type=jnp.float32
    )


def contract_cols(first_operand, second_operand):
    return lax.dot_general(
        first_operand, second_operand, (((1,), (1,)), ((), ())), preferred_element_type=jnp.float32
    )


def owned_strip(column_panel, shard_index, tensor_index, strip_width):
    block_width = column_panel.shape[1]
    first_index = shard_index * strip_width
    owner_index = first_index // block_width
    offset = jnp.clip(first_index - tensor_index * block_width, 0, block_width - strip_width)
    return (owner_index, lax.dynamic_slice_in_dim(column_panel, offset, strip_width, 1))


def per_device(gradient, moment, second_moment, stat_left, stat_right, basis_left, basis_right):
    shard_index = lax.axis_index("shard")
    tensor_index = lax.axis_index("tensor")
    rows_left = gradient.shape[0]
    rows_right = stat_right.shape[0]
    block_left = stat_left.shape[1]
    block_hidden = gradient.shape[1]
    moment_new = 0.9 * moment + 0.1 * gradient.astype(jnp.float32)
    moment_half = moment_new.astype(jnp.bfloat16)
    basis_left_half = basis_left.astype(jnp.bfloat16)
    basis_right_half = basis_right.astype(jnp.bfloat16)
    grad_rows, moment_rows, basis_left_rows = (
        lax.all_gather(gradient, "tensor", axis=1, tiled=True),
        lax.all_gather(moment_half, "tensor", axis=1, tiled=True),
        lax.all_gather(basis_left_half, "tensor", axis=1, tiled=True),
    )
    left_columns, right_columns = (
        lax.all_gather(basis_left_half, "shard", axis=0, tiled=True),
        lax.all_gather(basis_right_half, "shard", axis=0, tiled=True),
    )
    full_gradient = lax.all_gather(grad_rows, "shard", axis=0, tiled=True)
    own_rows = lax.dynamic_slice_in_dim(full_gradient, tensor_index * block_left, block_left, 0)
    cross_left = contract_cols(grad_rows, own_rows)
    gradient_strip = lax.dynamic_slice_in_dim(
        full_gradient, shard_index * rows_right, rows_right, 1
    )
    own_columns = lax.dynamic_slice_in_dim(
        full_gradient, tensor_index * block_hidden, block_hidden, 1
    )
    cross_right = contract_rows(gradient_strip, own_columns)
    stat_left_new = 0.95 * stat_left + 0.05 * cross_left
    stat_right_new = 0.95 * stat_right + 0.05 * cross_right
    stat_left_rows, stat_right_rows = (
        lax.all_gather(stat_left_new.astype(jnp.bfloat16), "tensor", axis=1, tiled=True),
        lax.all_gather(stat_right_new.astype(jnp.bfloat16), "tensor", axis=1, tiled=True),
    )
    power_left = matmul(stat_left_rows, left_columns)
    power_right = matmul(stat_right_rows, right_columns)
    square_left, square_right = lax.psum(
        (jnp.sum(power_left * power_left), jnp.sum(power_right * power_right)), ("shard", "tensor")
    )
    iterate_left = power_left / jnp.sqrt(square_left + 1e-06)
    iterate_right = power_right / jnp.sqrt(square_right + 1e-06)
    for iteration in range(NS_ITERS):
        left_half = iterate_left.astype(jnp.bfloat16)
        right_half = iterate_right.astype(jnp.bfloat16)
        left_panel, right_panel = (
            lax.all_gather(left_half, "shard", axis=0, tiled=True),
            lax.all_gather(right_half, "shard", axis=0, tiled=True),
        )
        gram_left = contract_cols(left_half, left_panel)
        gram_right = contract_cols(right_half, right_panel)
        gram_left, gram_right = lax.psum((gram_left, gram_right), "tensor")
        gram_left_half = gram_left.astype(jnp.bfloat16)
        gram_right_half = gram_right.astype(jnp.bfloat16)
        iterate_left = 1.5 * iterate_left - 0.5 * matmul(gram_left_half, left_panel)
        iterate_right = 1.5 * iterate_right - 0.5 * matmul(gram_right_half, right_panel)
    rotated_grad = matmul(grad_rows, right_columns).astype(jnp.bfloat16)
    rotated_moment = matmul(moment_rows, right_columns).astype(jnp.bfloat16)
    grad_panel, moment_panel = (
        lax.all_gather(rotated_grad, "shard", axis=0, tiled=True),
        lax.all_gather(rotated_moment, "shard", axis=0, tiled=True),
    )
    owner_left, local_left = owned_strip(left_columns, shard_index, tensor_index, rows_left)
    basis_strip = broadcast(local_left, "tensor", owner_left)
    grad_turned = contract_rows(basis_strip, grad_panel)
    moment_turned = contract_rows(basis_strip, moment_panel)
    second_new = 0.95 * second_moment + 0.05 * grad_turned * grad_turned
    scaled = (moment_turned / (jnp.sqrt(second_new) + 1e-08)).astype(jnp.bfloat16)
    back_terms = contract_cols(scaled, right_columns)
    back_half = lax.psum_scatter(back_terms, "tensor", scatter_dimension=1, tiled=True).astype(
        jnp.bfloat16
    )
    back_panel = lax.all_gather(back_half, "shard", axis=0, tiled=True)
    update = matmul(basis_left_rows, back_panel)
    return (
        update,
        moment_new,
        second_new,
        stat_left_new,
        stat_right_new,
        iterate_left,
        iterate_right,
    )


def solution(mesh):
    return jax.shard_map(
        per_device,
        mesh=mesh,
        in_specs=(
            P("shard", "tensor"),
            P("shard", "tensor"),
            P("shard", "tensor"),
            P("shard", "tensor"),
            P("shard", "tensor"),
            P("shard", "tensor"),
            P("shard", "tensor"),
        ),
        out_specs=(
            P("shard", "tensor"),
            P("shard", "tensor"),
            P("shard", "tensor"),
            P("shard", "tensor"),
            P("shard", "tensor"),
            P("shard", "tensor"),
            P("shard", "tensor"),
        ),
        check_vma=False,
    )
```

profile of v0, /device:TPU:1, one launch (start us, length us, event | category | flops | bytes accessed | tf_op | source)
XLA Modules:
  0.0 1062.2 jit_solution(13101491253910753219)
XLA Ops:
  7.2 1.6 convert_element_type.57
  8.9 9.0 all_gather.49
  18.0 124.4 %all-gather.17.cloned.1.call-done = bf16[3072,768]{1,0:T(8,128)(2,1)} async-done(((bf16[48,768]{1,0:T(8,128)(2,1)}), bf16[3072,768]{1,0:T(8,128)(2,1)}) %all-gather.17.cloned.1.call-update) | async-done | bytes 4718608 | tf_op jit(solution)/shard_map/all_gather | solution.py:56
  142.4 3.7 fusion.14
  146.8 9.3 all_gather.46
  156.1 3.7 fusion.13
  159.9 154.4 %all-gather = bf16[64,12,192]{2,1,0:T(8,128)(2,1)S(1)} all-gather(bf16[1,12,192]{2,1,0:T(8,128)(2,1)S(1)} %get-tuple-element.16), channel_id=1, replica_groups=mesh['shard'=64,'tensor'=4] {'shard'}, dimensions={0}, use_global_device_ids=true | all-gather | bytes 299520 | tf_op jit(solution)/shard_map/all_gather | solution.py:55
  314.6 40.0 %psum.49 = bf16[768,12]{1,0:T(8,128)(2,1)S(1)} all-reduce(bf16[768,12]{1,0:T(8,128)(2,1)S(1)} %dynamic-slice_select_fusion), channel_id=1, replica_groups=mesh['shard'=64,'tensor'=4] {'tensor'}, use_global_device_ids=true, to_apply=%region_0.0 | all-reduce | flops 9216 | bytes 36864 | tf_op jit(solution)/shard_map/psum | solution.py:11
  354.6 7.6 reshape.25
  362.3 1.7 fusion.22
  364.0 5.3 all-gather.6
  369.4 2.6 fusion.47
  372.0 8.4 all_gather.57
  380.4 3.8 multiply_reduce_fusion
  384.2 12.6 %all-gather.25.cloned.1.call-done = bf16[64,12,768]{2,1,0:T(8,128)(2,1)} async-done(((bf16[1,12,768]{2,1,0:T(8,128)(2,1)}), bf16[64,12,768]{2,1,0:T(8,128)(2,1)}) %all-gather.25.cloned.1.call-update) | async-done | bytes 1179664 | tf_op jit(solution)/shard_map/all_gather | solution.py:98
  396.8 2.2 reshape.19
  399.4 114.2 %all-gather.23.cloned.1.call-done = bf16[64,12,768]{2,1,0:T(8,128)(2,1)} async-done(((bf16[1,12,768]{2,1,0:T(8,128)(2,1)}), bf16[64,12,768]{2,1,0:T(8,128)(2,1)}) %all-gather.23.cloned.1.call-update) | async-done | bytes 1179664 | tf_op jit(solution)/shard_map/all_gather | solution.py:99
  513.6 2.2 reshape.17
  515.9 4.6 fusion.15
  521.3 78.2 %all-reduce = (f32[]{:T(128)}, f32[]{:T(128)}) all-reduce(f32[]{:T(128)} %get-tuple-element.17, f32[]{:T(128)} %get-tuple-element.21), channel_id=1, replica_groups=mesh['shard'=64,'tensor'=4] {'shard','tensor'}, use_global_device_ids=true, to_apply=%region_3.0 | all-reduce | flops 2 | bytes 16 | tf_op jit(solution)/shard_map/psum | solution.py:76
  601.0 1.4 convert_bitcast_fusion
  603.2 151.2 %all-gather.7 = bf16[64,12,192]{2,1,0:T(8,128)(2,1)S(1)} all-gather(bf16[1,12,192]{2,1,0:T(8,128)(2,1)S(1)} %fusion.45), channel_id=1, replica_groups=mesh['shard'=64,'tensor'=4] {'shard'}, dimensions={0}, use_global_device_ids=true | all-gather | bytes 299520 | tf_op jit(solution)/shard_map/all_gather | solution.py:85
  754.9 3.9 fusion.49
  758.7 44.7 %all-reduce.5 = (bf16[12,768]{1,0:T(8,128)(2,1)S(1)}, bf16[48,3072]{1,0:T(8,128)(2,1)S(1)}) all-reduce(f32[12,768]{1,0:T(8,128)S(1)} %fusion.43, f32[48,3072]{1,0:T(8,128)S(1)} %fusion.49), channel_id=1, replica_groups=mesh['shard'=64,'tensor'=4] {'tensor'}, use_global_device_ids=true, to_apply=%region_4.0 | all-reduce | flops 156672 | bytes 940032 | tf_op jit(solution)/shard_map/psum | solution.py:90
  803.5 3.9 fusion.48
  807.4 6.0 all-gather.4
  813.5 26.7 %all-gather.27.cloned.1.call-done = bf16[64,12,768]{2,1,0:T(8,128)(2,1)} async-done(((bf16[1,12,768]{2,1,0:T(8,128)(2,1)}), bf16[64,12,768]{2,1,0:T(8,128)(2,1)}) %all-gather.27.cloned.1.call-update) | async-done | bytes 1179664 | tf_op jit(solution)/shard_map/all_gather | solution.py:111
  840.3 2.2 reshape.21
  843.6 152.9 %all-gather.8 = bf16[64,12,192]{2,1,0:T(8,128)(2,1)S(1)} all-gather(bf16[1,12,192]{2,1,0:T(8,128)(2,1)S(1)} %convert_bitcast_fusion.2), channel_id=1, replica_groups=mesh['shard'=64,'tensor'=4] {'shard'}, dimensions={0}, use_global_device_ids=true | all-gather | bytes 299520 | tf_op jit(solution)/shard_map/all_gather | solution.py:85
  996.9 3.8 fusion.50
  1000.8 49.9 %all-reduce.6 = (bf16[12,768]{1,0:T(8,128)(2,1)S(1)}, bf16[48,3072]{1,0:T(8,128)(2,1)S(1)}) all-reduce(f32[12,768]{1,0:T(8,128)S(1)} %fusion.38, f32[48,3072]{1,0:T(8,128)S(1)} %fusion.50), channel_id=1, replica_groups=mesh['shard'=64,'tensor'=4] {'tensor'}, use_global_device_ids=true, to_apply=%region_5.0 | all-reduce | flops 156672 | bytes 940032 | tf_op jit(solution)/shard_map/psum | solution.py:90
  1051.5 3.9 fusion.4
  (61 shorter events, 6.2 us)
Async XLA Ops:
  7.2 139.0 %copy-start.4 = (bf16[12,768]{1,0:T(8,128)(2,1)S(1)}, bf16[12,768]{1,0:T(8,128)(2,1)}, u32[]{:S(2)}) copy-start(bf16[12,768]{1,0:T(8,128)(2,1)} %param.7) | copy-start | bytes 55300
  7.2 139.0 %copy-start.7 = (f32[12,768]{1,0:T(8,128)S(1)}, f32[12,768]{1,0:T(8,128)}, u32[]{:S(2)}) copy-start(f32[12,768]{1,0:T(8,128)} %param.8) | copy-start | bytes 110596
  7.2 135.2 %all-gather.17.cloned.1.call-start = ((), (), s32[]{:S(2)}) async-start(), calls=%async_computation.1 | async-start | bytes 4792320 | tf_op jit(solution)/shard_map/all_gather | solution.py:56
  8.8 345.8 %all-gather.29.cloned.1.call-start = ((), (), s32[]{:S(2)}) async-start(), calls=%async_computation.8 | async-start | bytes 6389760 | tf_op jit(solution)/shard_map/all_gather | solution.py:58
  17.9 141.9 %copy-start.9 = (f32[12,192]{1,0:T(8,128)S(1)}, f32[12,192]{1,0:T(8,128)}, u32[]{:S(2)}) copy-start(f32[12,192]{1,0:T(8,128)} %param.12) | copy-start | bytes 27652
  17.9 378.9 %all-gather.25.cloned.1.call-start = ((), (), s32[]{:S(2)}) async-start(), calls=%async_computation.6 | async-start | bytes 1597440 | tf_op jit(solution)/shard_map/all_gather | solution.py:98
  146.1 367.5 %all-gather.23.cloned.1.call-start = ((), (), s32[]{:S(2)}) async-start(), calls=%async_computation.5 | async-start | bytes 1597440 | tf_op jit(solution)/shard_map/all_gather | solution.py:99
  159.8 441.2 %reduce-scatter.2.cloned.1.call-start = ((), (), s32[]{:S(2)}) async-start(), calls=%async_computation.2 | async-start | bytes 245760 | tf_op jit(solution)/shard_map/reduce_scatter | solution.py:108
  354.6 7.7 copy-start
  354.6 7.7 copy-start.8
  354.6 14.8 %copy-start.3 = (f32[48,768]{1,0:T(8,128)S(1)}, f32[48,768]{1,0:T(8,128)}, u32[]{:S(2)}) copy-start(f32[48,768]{1,0:T(8,128)} %param.11) | copy-start | bytes 442372
  364.0 35.1 %copy-start.5 = (f32[12,192]{1,0:T(8,128)}, f32[12,192]{1,0:T(8,128)S(1)}, u32[]{:S(2)}) copy-start(f32[12,192]{1,0:T(8,128)S(1)} %fusion.22) | copy-start | bytes 27652
  369.4 29.7 %copy-start.6 = (f32[12,768]{1,0:T(8,128)S(1)}, f32[12,768]{1,0:T(8,128)}, u32[]{:S(2)}) copy-start(f32[12,768]{1,0:T(8,128)} %param.9) | copy-start | bytes 110596
  399.4 121.9 %copy-start.2 = (f32[12,768]{1,0:T(8,128)}, f32[12,768]{1,0:T(8,128)S(1)}, u32[]{:S(2)}) copy-start(f32[12,768]{1,0:T(8,128)S(1)} %fusion.31) | copy-start | bytes 110596
  520.5 234.4 %all-gather.19.cloned.1.call-start = ((), (), s32[]{:S(2)}) async-start(), calls=%async_computation.3 | async-start | bytes 4792320 | tf_op jit(solution)/shard_map/all_gather | solution.py:86
  600.9 239.4 %all-gather.27.cloned.1.call-start = ((), (), s32[]{:S(2)}) async-start(), calls=%async_computation.7 | async-start | bytes 1597440 | tf_op jit(solution)/shard_map/all_gather | solution.py:111
  602.4 394.5 %all-gather.21.cloned.1.call-start = ((), (), s32[]{:S(2)}) async-start(), calls=%async_computation.4 | async-start | bytes 4792320 | tf_op jit(solution)/shard_map/all_gather | solution.py:86
  807.4 189.5 %copy-start.1 = (bf16[48,768]{1,0:T(8,128)(2,1)S(1)}, bf16[48,768]{1,0:T(8,128)(2,1)}, u32[]{:S(2)}) copy-start(bf16[48,768]{1,0:T(8,128)(2,1)} %get-tuple-element.23) | copy-start | bytes 221188
Sparse Core Ops, SparseCore 0:
  12.2 130.0 all-gather.16
  146.0 134.3 all-gather.28
  284.7 112.0 all-gather.24
  400.9 112.6 all-gather.22
  520.6 20.4 reduce-scatter.1
  601.0 122.2 all-gather.18
  727.6 112.6 all-gather.26
  844.5 126.5 all-gather.20
where the time goes:
time: 1060 us
  blocking collectives  709 us (67%)
  waiting for transfers between devices  278 us (26%)
  matrix products  38.9 us (4%)
  between operations  15.9 us (2%)
  local copies, waits for them, and re-layouts  15.2 us (1%)
    all_gather x2, blocking collectives, per_device(): lax.all_gather(left_half, 'shard', axis=0, tiled=True)  304 us
    all_gather x1, blocking collectives, per_device(): lax.all_gather(basis_left_half, 'shard', axis=0, tiled=True)  154 us
    all_gather x1, waiting for transfers between devices, per_device(): lax.all_gather(basis_right_half, 'shard', axis=0, tiled=True)  124 us
    all_gather x1, waiting for transfers between devices, per_device(): lax.all_gather(rotated_moment, 'shard', axis=0, tiled=True)  114 us
    psum x2, blocking collectives, per_device(): gram_left, gram_right = lax.psum((gram_left, gram_right), 'tensor')  94.7 us
    psum x1, blocking collectives, per_device(): lax.psum((jnp.sum(power_left * power_left), jnp.sum(power_right * power_r...  78.2 us
    psum x1, blocking collectives, broadcast(): return lax.psum(jnp.where(mine, array, jnp.zeros_like(array)), axis)  40 us
    all_gather x1, waiting for transfers between devices, per_device(): back_panel = lax.all_gather(back_half, 'shard', axis=0, tiled=True)  26.7 us
  transfers between devices with their start and end apart: 8, of which 4 were waited for; matrix products, arithmetic and copies ran while one was open for 4% of the time, Pallas kernels for 0%

commit v1 on v0

--- a/solution.py
+++ b/solution.py
@@ -96,7 +96,10 @@
     rotated_moment = matmul(moment_rows, right_columns).astype(jnp.bfloat16)
     grad_panel, moment_panel = (
         lax.all_gather(rotated_grad, "shard", axis=0, tiled=True),
-        lax.all_gather(rotated_moment, "shard", axis=0, tiled=True),
+        jnp.concatenate(
+            lax.all_to_all(jnp.stack([rotated_moment] * lax.axis_size("shard")), "shard", 0, 0),
+            axis=0,
+        ),
     )
     owner_left, local_left = owned_strip(left_columns, shard_index, tensor_index, rows_left)
     basis_strip = broadcast(local_left, "tensor", owner_left)

time: 1060 us -> 959 us (0.905)
  waiting for transfers between devices: 278 us -> 141 us
  blocking collectives: 709 us -> 733 us
    all_gather x1 -> x0, waiting for transfers between devices: 114 us -> none  [per_device(): lax.all_gather(rotated_moment, 'shard', axis=0, tiled=True)]
    all_gather x1, blocking collectives: 154 us -> 181 us  [per_device(): lax.all_gather(basis_left_half, 'shard', axis=0, tiled=True)]
    all_gather x1, waiting for transfers between devices: 12.6 us -> 0.01 us  [per_device(): lax.all_gather(rotated_grad, 'shard', axis=0, tiled=True)]
  transfers between devices with their start and end apart: 8 -> 8, of which waited for: 4 -> 2; matrix products, arithmetic and copies ran while one was open for 4% -> 5% of each run, Pallas kernels for 0% -> 0%
where the time goes in v1:
time: 959 us; the launch traced here: 958 us
  blocking collectives  733 us (76%)
  waiting for transfers between devices  141 us (15%)
  matrix products  39.2 us (4%)
  between operations  15.8 us (2%)
  local copies, waits for them, and re-layouts  15.2 us (2%)
    all_gather x2, blocking collectives, per_device(): lax.all_gather(left_half, 'shard', axis=0, tiled=True)  305 us
    all_gather x1, blocking collectives, per_device(): lax.all_gather(basis_left_half, 'shard', axis=0, tiled=True)  181 us
    all_gather x1, waiting for transfers between devices, per_device(): lax.all_gather(basis_right_half, 'shard', axis=0, tiled=True)  118 us
    psum x2, blocking collectives, per_device(): gram_left, gram_right = lax.psum((gram_left, gram_right), 'tensor')  95.2 us
    psum x1, blocking collectives, per_device(): lax.psum((jnp.sum(power_left * power_left), jnp.sum(power_right * power_r...  72.8 us
    psum x1, blocking collectives, broadcast(): return lax.psum(jnp.where(mine, array, jnp.zeros_like(array)), axis)  45.8 us
    all_gather x1, waiting for transfers between devices, per_device(): back_panel = lax.all_gather(back_half, 'shard', axis=0, tiled=True)  22.8 us
    dot_general x9, matrix products, matmul(): jnp.dot(first_operand, second_operand, preferred_element_type=jnp.float32)  21 us
  transfers between devices with their start and end apart: 8, of which 2 were waited for; matrix products, arithmetic and copies ran while one was open for 5% of the time, Pallas kernels for 0%

profile of v1, /device:TPU:1, one launch (start us, length us, event | category | flops | bytes accessed | tf_op | source)
XLA Modules:
  0.0 957.8 jit_solution(121721321244660583)
XLA Ops:
  7.2 1.6 convert_element_type.57
  8.8 9.0 all_gather.45
  17.9 1.4 fusion.45
  19.4 5.3 all_gather.43
  24.7 117.7 %all-gather.15.cloned.1.call-done = bf16[3072,768]{1,0:T(8,128)(2,1)} async-done(((bf16[48,768]{1,0:T(8,128)(2,1)}), bf16[3072,768]{1,0:T(8,128)(2,1)}) %all-gather.15.cloned.1.call-update) | async-done | bytes 4718608 | tf_op jit(solution)/shard_map/all_gather | solution.py:56
  142.3 3.7 fusion.13
  146.1 3.1 convolution_convert_fusion.1
  149.2 1.3 stack.2
  150.5 8.0 all-to-all-start
  159.2 181.2 %all-gather = bf16[64,12,192]{2,1,0:T(8,128)(2,1)S(1)} all-gather(bf16[1,12,192]{2,1,0:T(8,128)(2,1)S(1)} %get-tuple-element.16), channel_id=1, replica_groups=mesh['shard'=64,'tensor'=4] {'shard'}, dimensions={0}, use_global_device_ids=true | all-gather | bytes 299520 | tf_op jit(solution)/shard_map/all_gather | solution.py:55
  340.8 45.8 %psum.49 = bf16[768,12]{1,0:T(8,128)(2,1)S(1)} all-reduce(bf16[768,12]{1,0:T(8,128)(2,1)S(1)} %dynamic-slice_select_fusion), channel_id=1, replica_groups=mesh['shard'=64,'tensor'=4] {'tensor'}, use_global_device_ids=true, to_apply=%region_0.0 | all-reduce | flops 9216 | bytes 36864 | tf_op jit(solution)/shard_map/psum | solution.py:11
  386.7 7.7 reshape.29
  394.4 1.7 fusion.21
  396.1 6.1 all-gather.5
  402.9 2.6 fusion.46
  405.5 6.0 all_gather.53
  411.5 3.8 multiply_reduce_fusion
  415.4 2.2 reshape.23
  419.1 4.6 fusion.14
  424.5 72.8 %all-reduce = (f32[]{:T(128)}, f32[]{:T(128)}) all-reduce(f32[]{:T(128)} %get-tuple-element.17, f32[]{:T(128)} %get-tuple-element.21), channel_id=1, replica_groups=mesh['shard'=64,'tensor'=4] {'shard','tensor'}, use_global_device_ids=true, to_apply=%region_3.0 | all-reduce | flops 2 | bytes 16 | tf_op jit(solution)/shard_map/psum | solution.py:76
  498.7 1.4 convert_bitcast_fusion
  500.9 152.5 %all-gather.6 = bf16[64,12,192]{2,1,0:T(8,128)(2,1)S(1)} all-gather(bf16[1,12,192]{2,1,0:T(8,128)(2,1)S(1)} %fusion.44), channel_id=1, replica_groups=mesh['shard'=64,'tensor'=4] {'shard'}, dimensions={0}, use_global_device_ids=true | all-gather | bytes 299520 | tf_op jit(solution)/shard_map/all_gather | solution.py:85
  653.8 3.9 fusion.48
  657.7 45.4 %all-reduce.5 = (bf16[12,768]{1,0:T(8,128)(2,1)S(1)}, bf16[48,3072]{1,0:T(8,128)(2,1)S(1)}) all-reduce(f32[12,768]{1,0:T(8,128)S(1)} %fusion.42, f32[48,3072]{1,0:T(8,128)S(1)} %fusion.48), channel_id=1, replica_groups=mesh['shard'=64,'tensor'=4] {'tensor'}, use_global_device_ids=true, to_apply=%region_4.0 | all-reduce | flops 156672 | bytes 940032 | tf_op jit(solution)/shard_map/psum | solution.py:90
  703.1 3.9 fusion.47
  707.0 6.0 all-gather.3
  713.1 22.8 %all-gather.23.cloned.1.call-done = bf16[64,12,768]{2,1,0:T(8,128)(2,1)} async-done(((bf16[1,12,768]{2,1,0:T(8,128)(2,1)}), bf16[64,12,768]{2,1,0:T(8,128)(2,1)}) %all-gather.23.cloned.1.call-update) | async-done | bytes 1179664 | tf_op jit(solution)/shard_map/all_gather | solution.py:114
  735.9 2.2 reshape.25
  739.3 152.9 %all-gather.7 = bf16[64,12,192]{2,1,0:T(8,128)(2,1)S(1)} all-gather(bf16[1,12,192]{2,1,0:T(8,128)(2,1)S(1)} %convert_bitcast_fusion.2), channel_id=1, replica_groups=mesh['shard'=64,'tensor'=4] {'shard'}, dimensions={0}, use_global_device_ids=true | all-gather | bytes 299520 | tf_op jit(solution)/shard_map/all_gather | solution.py:85
  892.6 3.8 fusion.49
  896.4 49.8 %all-reduce.6 = (bf16[12,768]{1,0:T(8,128)(2,1)S(1)}, bf16[48,3072]{1,0:T(8,128)(2,1)S(1)}) all-reduce(f32[12,768]{1,0:T(8,128)S(1)} %fusion.37, f32[48,3072]{1,0:T(8,128)S(1)} %fusion.49), channel_id=1, replica_groups=mesh['shard'=64,'tensor'=4] {'tensor'}, use_global_device_ids=true, to_apply=%region_5.0 | all-reduce | flops 156672 | bytes 940032 | tf_op jit(solution)/shard_map/psum | solution.py:90
  947.1 3.9 fusion.4
  (59 shorter events, 7.8 us)
Async XLA Ops:
  7.2 135.2 %all-gather.15.cloned.1.call-start = ((), (), s32[]{:S(2)}) async-start(), calls=%async_computation.2 | async-start | bytes 4792320 | tf_op jit(solution)/shard_map/all_gather | solution.py:56
  8.8 377.9 %all-gather.25.cloned.1.call-start = ((), (), s32[]{:S(2)}) async-start(), calls=%async_computation.8 | async-start | bytes 6389760 | tf_op jit(solution)/shard_map/all_gather | solution.py:58
  17.9 397.5 %all-gather.21.cloned.1.call-start = ((), (), s32[]{:S(2)}) async-start(), calls=%async_computation.6 | async-start | bytes 1597440 | tf_op jit(solution)/shard_map/all_gather | solution.py:98
  146.1 12.5 %copy-start.8 = (f32[12,192]{1,0:T(8,128)S(1)}, f32[12,192]{1,0:T(8,128)}, u32[]{:S(2)}) copy-start(f32[12,192]{1,0:T(8,128)} %param.12) | copy-start | bytes 27652
  150.5 268.3 %all-to-all-start = ((bf16[64,12,768]{2,1,0:T(8,128)(2,1)}), bf16[64,12,768]{2,1,0:T(8,128)(2,1)S(1)}, u32[]{:S(2)}, u32[]{:S(2)}) async-start(bf16[64,12,768]{2,1,0:T(8,128)(2,1)} %stack.2), calls=%async_computation | async-start | bytes 3145728 | tf_op jit(solution)/shard_map/all_to_all | solution.py:100
  158.5 340.2 %reduce-scatter.2.cloned.1.call-start = ((), (), s32[]{:S(2)}) async-start(), calls=%async_computation.3 | async-start | bytes 245760 | tf_op jit(solution)/shard_map/reduce_scatter | solution.py:111
  386.6 7.7 copy-start
  386.6 7.7 copy-start.7
  386.6 16.2 %copy-start.3 = (f32[48,768]{1,0:T(8,128)S(1)}, f32[48,768]{1,0:T(8,128)}, u32[]{:S(2)}) copy-start(f32[48,768]{1,0:T(8,128)} %param.11) | copy-start | bytes 442372
  396.0 21.6 %copy-start.5 = (f32[12,192]{1,0:T(8,128)}, f32[12,192]{1,0:T(8,128)S(1)}, u32[]{:S(2)}) copy-start(f32[12,192]{1,0:T(8,128)S(1)} %fusion.21) | copy-start | bytes 27652
  418.7 5.8 copy-start.2
  419.1 4.7 copy-start.4
  423.7 230.1 %all-gather.17.cloned.1.call-start = ((), (), s32[]{:S(2)}) async-start(), calls=%async_computation.4 | async-start | bytes 4792320 | tf_op jit(solution)/shard_map/all_gather | solution.py:86
  498.7 237.3 %all-gather.23.cloned.1.call-start = ((), (), s32[]{:S(2)}) async-start(), calls=%async_computation.7 | async-start | bytes 1597440 | tf_op jit(solution)/shard_map/all_gather | solution.py:114
  500.2 392.4 %all-gather.19.cloned.1.call-start = ((), (), s32[]{:S(2)}) async-start(), calls=%async_computation.5 | async-start | bytes 4792320 | tf_op jit(solution)/shard_map/all_gather | solution.py:86
  653.8 53.2 %copy-start.6 = (bf16[1,192,12]{1,2,0:T(8,128)(2,1)S(1)}, bf16[1,192,12]{1,2,0:T(8,128)(2,1)}, u32[]{:S(2)}) copy-start(bf16[1,192,12]{1,2,0:T(8,128)(2,1)} %get-tuple-element.15) | copy-start | bytes 13828
  707.0 185.6 %copy-start.1 = (bf16[48,768]{1,0:T(8,128)(2,1)S(1)}, bf16[48,768]{1,0:T(8,128)(2,1)}, u32[]{:S(2)}) copy-start(bf16[48,768]{1,0:T(8,128)(2,1)} %get-tuple-element.23) | copy-start | bytes 221188
Sparse Core Ops, SparseCore 0:
  12.2 130.0 all-gather.14
  146.0 136.9 all-gather.24
  287.2 113.6 all-gather.20
  423.8 11.7 reduce-scatter.1
  498.8 120.7 all-gather.16
  623.7 112.1 all-gather.22
  740.2 126.5 all-gather.18
